TPU v7x, 256 devices: a whole 4x4x8 slice. The times are simulated.
256 devices in a mesh: grp: 2 (over core), mr: 16 (over y_lo, z), mc: 8 (over y_hi, x).
Axes of the slice: x: 4, y: 4 (y_hi: 2, y_lo: 2; y = y_hi * 2 + y_lo), z: 8, core: 2. Of those that a mesh axis runs over, the one named last changes fastest.
Arguments:
- queries: bfloat16 [768, 8192], P(('grp', 'mr'), 'mc'), may hold values from -6 to 6
- new_keys: bfloat16 [768, 1024], P(('grp', 'mr'), 'mc'), may hold values from -6 to 6
- new_values: bfloat16 [768, 1024], P(('grp', 'mr'), 'mc'), may hold values from -6 to 6
- key_cache: bfloat16 [768, 512, 1024], P(('grp', 'mr'), None, 'mc'), may hold values from -6 to 6
- value_cache: bfloat16 [768, 512, 1024], P(('grp', 'mr'), None, 'mc'), may hold values from -6 to 6
- context_len: int32 [768], P(('grp', 'mr')), may hold values from 2 to 512, as said below
- cache_slot: int32 [768], P(('grp', 'mr')), may hold values from 0 to 767, as said below
- residual_in: bfloat16 [768, 8192], P(('grp', 'mr'), 'mc'), may hold values from -31 to 31
- out_weight: bfloat16 [8192, 8192], P(('grp', 'mr'), 'mc'), may hold values from -0.25 to 0.25
- gate_weight: bfloat16 [8192, 28672], P('mc', ('grp', 'mr')), may hold values from -0.0625 to 0.0625
- up_weight: bfloat16 [8192, 28672], P('mc', ('grp', 'mr')), may hold values from -0.0625 to 0.0625
Outputs:
- residual_out: bfloat16 [768, 8192], P(('grp', 'mr'), 'mc')
- activation: bfloat16 [768, 28672], P('mc', ('grp', 'mr'))
Inputs may be any that keep to these rules, and one draw needn't show every extreme that they name: Row r's history fills positions 0 to context_len[r] - 1 of its cache row; some row has 512. `cache_slot`: within each aligned block of 24 rows the values are a permutation of that block's own row indices.
All inputs are finite; a program needn't handle non-finite values.
Results may differ from a plain program's by a relative error of at most 0.006.
Values may be sent and summed in bfloat16 or wider, within the bound.
No kernel may reach another device: no remote copies, remote signals or barrier semaphores. Data moves between devices by JAX's collectives and lax.ppermute only.
A program may use at most 64 MiB of HBM per device.

v0:
```python
import math
import jax
import jax.numpy as jnp
from jax import lax
from jax.sharding import PartitionSpec as P

D = 8192
HD = 128
norm_epsilon = 1e-05
masked_score = -1e30


def copy_for_each(shard, axis):
    devices = lax.axis_size(axis)
    return lax.all_to_all(
        jnp.broadcast_to(shard[None], (devices, *shard.shape)), axis, 0, 0, tiled=True
    )


def in_order(parts, dim):
    parts = jnp.moveaxis(parts, 0, dim)
    dims = parts.shape
    return parts.reshape(*dims[:dim], dims[dim] * dims[dim + 1], *dims[dim + 2 :])


def collect(shard, axis, dim):
    parts = copy_for_each(shard, axis)
    return in_order(parts, dim)


def side_by_side(arrays, axis, dim, along):
    widths = [math.prod(a.shape[along:]) for a in arrays]
    both = jnp.concatenate(
        [a.reshape(*a.shape[:along], w) for a, w in zip(arrays, widths)], axis=along
    )
    filled = lax.psum_scatter(both, axis, scatter_dimension=dim, tiled=True)
    parts = jnp.split(filled, [sum(widths[:k]) for k in range(1, len(widths))], axis=along)
    return tuple(
        (b.reshape(*filled.shape[:along], *a.shape[along:]) for a, b in zip(arrays, parts))
    )


def attend_rows(queries, new_keys, new_values, key_rows, value_rows, context_len):
    row_denominator_sum = queries.shape[0]
    context = key_rows.shape[1]
    kv_heads = key_rows.shape[2] // HD
    groups = queries.shape[1] // key_rows.shape[2]
    attention_logit_scale = HD ** (-0.5)
    query_grouped_four = queries.reshape(row_denominator_sum, kv_heads, groups, HD)
    key_four = key_rows.reshape(row_denominator_sum, context, kv_heads, HD)
    value_four = value_rows.reshape(row_denominator_sum, context, kv_heads, HD)
    current_key = new_keys.reshape(row_denominator_sum, kv_heads, HD)
    own_value = new_values.reshape(row_denominator_sum, kv_heads, HD).astype(jnp.float32)
    scores = (
        jnp.einsum(
            "bkgd,bckd->bkgc", query_grouped_four, key_four, preferred_element_type=jnp.float32
        )
        * attention_logit_scale
    )
    positions = jnp.arange(context, dtype=jnp.int32)
    valid_mask = positions[None, :] < context_len[:, None]
    scores = jnp.where(valid_mask[:, None, None, :], scores, masked_score)
    current_score = (
        jnp.einsum(
            "cnhz,cnz->cnh", query_grouped_four, current_key, preferred_element_type=jnp.float32
        )
        * attention_logit_scale
    )
    row_max = jnp.maximum(jnp.max(scores, axis=3), current_score)
    exponent = jnp.exp(scores - row_max[..., None])
    own_exponent = jnp.exp(current_score - row_max)
    denominator = jnp.sum(exponent, axis=3) + own_exponent
    weights = (exponent / denominator[..., None]).astype(jnp.bfloat16)
    own_weight = (own_exponent / denominator).astype(jnp.bfloat16).astype(jnp.float32)
    combined = jnp.einsum(
        "bkgc,bckd->bkgd", weights, value_four, preferred_element_type=jnp.float32
    )
    combined = combined + own_weight[..., None] * own_value[:, :, None, :]
    return combined.reshape(row_denominator_sum, -1).astype(jnp.bfloat16)


def body(
    queries,
    new_keys,
    new_values,
    key_cache,
    value_cache,
    context_len,
    cache_slot,
    residual_in,
    out_weight,
    gate_weight,
    up_weight,
):
    local_rows = queries.shape[0]
    row_base = lax.axis_index(("grp", "mr")) * local_rows
    device_slot_index = cache_slot - row_base
    positions = jnp.arange(local_rows, dtype=jnp.int32)
    matches = device_slot_index[:, None] == positions[None, :]
    inverse = jnp.sum(jnp.where(matches, positions[:, None], 0), axis=0)
    by_cache = attend_rows(
        jnp.take(queries, inverse, axis=0),
        jnp.take(new_keys, inverse, axis=0),
        jnp.take(new_values, inverse, axis=0),
        key_cache,
        value_cache,
        jnp.take(context_len, inverse, axis=0),
    )
    attended = jnp.take(by_cache, device_slot_index, axis=0)
    gathered = collect(attended, "mc", 1)
    features = lax.all_to_all(gathered, ("grp", "mr"), split_axis=1, concat_axis=0, tiled=True)
    partial_value = jnp.dot(features, out_weight, preferred_element_type=jnp.float32)
    own_rows = lax.dynamic_slice_in_dim(partial_value, row_base, local_rows) + residual_in.astype(
        jnp.float32
    )
    partial_value = lax.dynamic_update_slice_in_dim(partial_value, own_rows, row_base, 0)
    summed = lax.psum(partial_value, ("grp", "mr"))
    everyone = summed.astype(jnp.bfloat16)
    residual_out = lax.dynamic_slice_in_dim(everyone, row_base, local_rows)
    widened = lax.optimization_barrier(everyone).astype(jnp.float32)
    squares = jnp.sum(widened * widened, axis=1)
    gate_term = jnp.dot(everyone, gate_weight, preferred_element_type=jnp.float32)
    up_term = jnp.dot(everyone, up_weight, preferred_element_type=jnp.float32)
    gate_sum, up_sum, square_sum = side_by_side((gate_term, up_term, squares), "mc", 0, 1)
    inverse_rms = lax.rsqrt(square_sum / D + norm_epsilon)
    gate_value = gate_sum * inverse_rms[:, None]
    upward = up_sum * inverse_rms[:, None]
    activation = (jax.nn.silu(gate_value) * upward).astype(jnp.bfloat16)
    return (residual_out, activation)


def solution(mesh):
    in_specs = (
        P(("grp", "mr"), "mc"),
        P(("grp", "mr"), "mc"),
        P(("grp", "mr"), "mc"),
        P(("grp", "mr"), None, "mc"),
        P(("grp", "mr"), None, "mc"),
        P(("grp", "mr")),
        P(("grp", "mr")),
        P(("grp", "mr"), "mc"),
        P(("grp", "mr"), "mc"),
        P("mc", ("grp", "mr")),
        P("mc", ("grp", "mr")),
    )
    out_specs = (P(("grp", "mr"), "mc"), P("mc", ("grp", "mr")))
    return jax.shard_map(body, mesh=mesh, in_specs=in_specs, out_specs=out_specs, check_vma=False)
```

profile of v0, /device:TPU:1, one launch (start us, length us, event | category | flops | bytes accessed | tf_op | source)
XLA Modules:
  0.0 330.5 jit_solution(5667355430699239794)
XLA Ops:
  7.2 0.8 compare_and_fusion
  8.1 1.4 gather_fusion
  9.5 1.3 gather_fusion.3
  10.8 1.3 gather_fusion.2
  12.1 1.4 gather_fusion.1
  13.9 1.0 fusion.15
  15.5 0.6 fusion.1
  16.1 0.6 gather_fusion.4
  16.8 16.8 %all_to_all.24 = bf16[8,24,1024]{2,1,0:T(8,128)(2,1)S(1)} all-to-all(bf16[8,24,1024]{2,1,0:T(8,128)(2,1)S(1)} %broadcast_in_dim.66), channel_id=1, replica_groups=mesh['grp'=2,'mr'=16,'mc'=8] {'mc'}, dimensions={0} | all-to-all | bytes 786432 | tf_op jit(solution)/shard_map/all_to_all | solution.py:15
  33.9 1.0 all_to_all.18
  34.8 2.0 copy.19
  36.8 10.3 %all-to-all-start.1 = ((bf16[24,32,256]{2,0,1:T(8,128)(2,1)}), bf16[24,32,256]{2,0,1:T(8,128)(2,1)S(1)}, u32[]{:S(2)}, u32[]{:S(2)}) async-start(bf16[24,32,256]{2,0,1:T(8,128)(2,1)} %copy.19), calls=%async_computation.1 | async-start | bytes 786432 | tf_op jit(solution)/shard_map/all_to_all | solution.py:111
  47.2 13.3 %all-to-all-done.1 = bf16[24,32,256]{2,0,1:T(8,128)(2,1)S(1)} async-done(((bf16[24,32,256]{2,0,1:T(8,128)(2,1)}), bf16[24,32,256]{2,0,1:T(8,128)(2,1)S(1)}, u32[]{:S(2)}, u32[]{:S(2)}) %all-to-all-start.1) | async-done | bytes 393248 | tf_op jit(solution)/shard_map/all_to_all | solution.py:111
  60.5 3.3 fusion.16
  63.8 1.5 add_dynamic-update-slice_fusion
  65.3 145.9 %all-reduce.1 = bf16[768,1024]{1,0:T(8,128)(2,1)} all-reduce(f32[768,1024]{1,0:T(8,128)} %add_dynamic-update-slice_fusion), channel_id=1, replica_groups=mesh['grp'=2,'mr'=16,'mc'=8] {'grp','mr'}, use_global_device_ids=true, to_apply=%region_3.6 | all-reduce | flops 786432 | bytes 4718592 | tf_op jit(solution)/shard_map/psum | solution.py:117
  211.2 1.8 multiply_reduce_fusion
  213.2 3.9 %fusion.18 = f32[768,896]{1,0:T(8,128)S(1)} fusion(bf16[768,1024]{1,0:T(8,128)(2,1)} %all-reduce.1, bf16[1024,896]{1,0:T(8,128)(2,1)} %param.25), kind=kOutput, calls=%fused_computation.55 | convolution fusion | flops 1409286144 | bytes 6160384 | tf_op jit(solution)/shard_map/dot_general | solution.py:123
  217.1 1.8 fusion.17
  218.9 2.9 pad_maximum_fusion
  221.8 1.4 constant_dynamic-slice_fusion
  223.2 97.5 %reduce-scatter.2.cloned.1.call-done = f32[96,1793]{1,0:T(8,128)} async-done(((f32[768,1793]{1,0:T(8,128)}), f32[96,1793]{1,0:T(8,128)}) %reduce-scatter.2.cloned.1.call-update) | async-done | bytes 688528 | tf_op jit(solution)/shard_map/reduce_scatter | solution.py:36
  320.8 0.9 fusion.9
  321.7 1.9 fusion.4
  (31 shorter events, 1.7 us)
Async XLA Ops:
  7.2 6.7 %copy-start = (bf16[24,512,128]{2,1,0:T(8,128)(2,1)S(1)}, bf16[24,512,128]{2,1,0:T(8,128)(2,1)}, u32[]{:S(2)}) copy-start(bf16[24,512,128]{2,1,0:T(8,128)(2,1)} %param.18) | copy-start | bytes 9437188
  13.6 1.9 copy-start.2
  36.8 23.7 %all-to-all-start.1 = ((bf16[24,32,256]{2,0,1:T(8,128)(2,1)}), bf16[24,32,256]{2,0,1:T(8,128)(2,1)S(1)}, u32[]{:S(2)}, u32[]{:S(2)}) async-start(bf16[24,32,256]{2,0,1:T(8,128)(2,1)} %copy.19), calls=%async_computation.1 | async-start | bytes 786432 | tf_op jit(solution)/shard_map/all_to_all | solution.py:111
  47.1 273.6 %reduce-scatter.2.cloned.1.call-start = ((), (), s32[]{:S(2)}) async-start(), calls=%async_computation.3 | async-start | bytes 6635520 | tf_op jit(solution)/shard_map/reduce_scatter | solution.py:36
  60.5 3.3 copy-start.3
  213.2 3.9 %copy-start.1 = (bf16[768,1024]{1,0:T(8,128)(2,1)S(1)}, bf16[768,1024]{1,0:T(8,128)(2,1)}, u32[]{:S(2)}) copy-start(bf16[768,1024]{1,0:T(8,128)(2,1)} %all-reduce.1) | copy-start | bytes 4718596
  213.2 3.9 %copy-start.4 = (bf16[1024,896]{1,0:T(8,128)(2,1)S(1)}, bf16[1024,896]{1,0:T(8,128)(2,1)}, u32[]{:S(2)}) copy-start(bf16[1024,896]{1,0:T(8,128)(2,1)} %param.24) | copy-start | bytes 5505028
Sparse Core Ops, SparseCore 0:
  221.9 98.8 reduce-scatter.1
where the time goes:
time: 331 us; the launch traced here: 330 us
  blocking collectives  163 us (49%)
  waiting for transfers between devices  111 us (34%)
  between operations  14.2 us (4%)
  local copies, waits for them, and re-layouts  11.1 us (3%)
  matrix products  10.7 us (3%)
  other arithmetic  10.5 us (3%)
  starting transfers between devices  10.4 us (3%)
    psum x1, blocking collectives, body(): summed = lax.psum(partial_value, ('grp', 'mr'))  146 us
    reduce_scatter x1, waiting for transfers between devices, side_by_side(): filled = lax.psum_scatter(both, axis, scatter_dimension=dim, tiled=True)  97.5 us
    all_to_all x1, blocking collectives, copy_for_each(): lax.all_to_all(jnp.broadcast_to(shard[None], (devices, *shard.shape)), ax...  16.8 us
    all_to_all x1, waiting for transfers between devices, body(): lax.all_to_all(gathered, ('grp', 'mr'), split_axis=1, concat_axis=0, tile...  13.3 us
    all_to_all x1, starting transfers between devices, body(): lax.all_to_all(gathered, ('grp', 'mr'), split_axis=1, concat_axis=0, tile...  10.3 us
  transfers between devices with their start and end apart: 2, of which 2 were waited for; matrix products, arithmetic and copies ran while one was open for 0% of the time, Pallas kernels for 0%

commit v1 on v0

--- a/solution.py
+++ b/solution.py
@@ -114,7 +114,7 @@
         jnp.float32
     )
     partial_value = lax.dynamic_update_slice_in_dim(partial_value, own_rows, row_base, 0)
-    summed = lax.psum(partial_value, ("grp", "mr"))
+    summed = lax.psum(lax.psum(partial_value, "grp"), "mr")
     everyone = summed.astype(jnp.bfloat16)
     residual_out = lax.dynamic_slice_in_dim(everyone, row_base, local_rows)
     widened = lax.optimization_barrier(everyone).astype(jnp.float32)

time: 331 us -> 300 us (0.906)
  blocking collectives: 163 us -> 93 us
  waiting for transfers between devices: 111 us -> 150 us
    psum x1, blocking collectives: 146 us -> 76.1 us  [body(): summed = lax.psum(lax.psum(partial_value, 'grp'), 'mr')]
    psum x0 -> x1, waiting for transfers between devices: none -> 30 us  [body(): summed = lax.psum(lax.psum(partial_value, 'grp'), 'mr')]
    reduce_scatter x1, waiting for transfers between devices: 97.5 us -> 106 us  [side_by_side(): filled = lax.psum_scatter(both, axis, scatter_dimension=dim, tiled=True)]
  transfers between devices with their start and end apart: 2 -> 3, of which waited for: 2 -> 3; matrix products, arithmetic and copies ran while one was open for 0% -> 0% of each run, Pallas kernels for 0% -> 0%
where the time goes in v1:
time: 300 us
  waiting for transfers between devices  150 us (50%)
  blocking collectives  93 us (31%)
  between operations  14.2 us (5%)
  local copies, waits for them, and re-layouts  11.1 us (4%)
  matrix products  10.7 us (4%)
  other arithmetic  10.5 us (4%)
  starting transfers between devices  10.4 us (3%)
    reduce_scatter x1, waiting for transfers between devices, side_by_side(): filled = lax.psum_scatter(both, axis, scatter_dimension=dim, tiled=True)  106 us
    psum x1, blocking collectives, body(): summed = lax.psum(lax.psum(partial_value, 'grp'), 'mr')  76.1 us
    psum x1, waiting for transfers between devices, body(): summed = lax.psum(lax.psum(partial_value, 'grp'), 'mr')  30 us
    all_to_all x1, blocking collectives, copy_for_each(): lax.all_to_all(jnp.broadcast_to(shard[None], (devices, *shard.shape)), ax...  16.8 us
    all_to_all x1, waiting for transfers between devices, body(): lax.all_to_all(gathered, ('grp', 'mr'), split_axis=1, concat_axis=0, tile...  13.3 us
    all_to_all x1, starting transfers between devices, body(): lax.all_to_all(gathered, ('grp', 'mr'), split_axis=1, concat_axis=0, tile...  10.3 us
  transfers between devices with their start and end apart: 3, of which 3 were waited for; matrix products, arithmetic and copies ran while one was open for 0% of the time, Pallas kernels for 0%

profile of v1, /device:TPU:1, one launch (start us, length us, event | category | flops | bytes accessed | tf_op | source)
XLA Modules:
  0.0 299.6 jit_solution(934054599703709750)
XLA Ops:
  7.2 0.8 compare_and_fusion
  8.1 1.4 gather_fusion
  9.5 1.3 gather_fusion.3
  10.8 1.3 gather_fusion.2
  12.1 1.4 gather_fusion.1
  13.9 1.0 fusion.15
  16.1 0.6 gather_fusion.4
  16.8 16.8 %all_to_all.24 = bf16[8,24,1024]{2,1,0:T(8,128)(2,1)S(1)} all-to-all(bf16[8,24,1024]{2,1,0:T(8,128)(2,1)S(1)} %broadcast_in_dim.66), channel_id=1, replica_groups=mesh['grp'=2,'mr'=16,'mc'=8] {'mc'}, dimensions={0} | all-to-all | bytes 786432 | tf_op jit(solution)/shard_map/all_to_all | solution.py:15
  33.9 1.0 all_to_all.18
  34.8 2.0 copy.19
  36.8 10.3 %all-to-all-start.1 = ((bf16[24,32,256]{2,0,1:T(8,128)(2,1)}), bf16[24,32,256]{2,0,1:T(8,128)(2,1)S(1)}, u32[]{:S(2)}, u32[]{:S(2)}) async-start(bf16[24,32,256]{2,0,1:T(8,128)(2,1)} %copy.19), calls=%async_computation.1 | async-start | bytes 786432 | tf_op jit(solution)/shard_map/all_to_all | solution.py:111
  47.2 13.3 %all-to-all-done.1 = bf16[24,32,256]{2,0,1:T(8,128)(2,1)S(1)} async-done(((bf16[24,32,256]{2,0,1:T(8,128)(2,1)}), bf16[24,32,256]{2,0,1:T(8,128)(2,1)S(1)}, u32[]{:S(2)}, u32[]{:S(2)}) %all-to-all-start.1) | async-done | bytes 393248 | tf_op jit(solution)/shard_map/all_to_all | solution.py:111
  60.5 3.3 %fusion.16 = f32[768,1024]{1,0:T(8,128)} fusion(bf16[768,256]{1,0:T(8,128)(2,1)S(1)} %bitcast.31, bf16[256,1024]{1,0:T(8,128)(2,1)} %param.23), kind=kOutput, calls=%fused_computation.53 | convolution fusion | flops 402653184 | bytes 4063232 | tf_op jit(solution)/shard_map/dot_general | solution.py:112
  63.8 1.5 add_dynamic-update-slice_fusion
  65.4 30.0 %all-reduce.3.cloned.1.call-done = f32[768,1024]{1,0:T(8,128)} async-done(((f32[768,1024]{1,0:T(8,128)}), f32[768,1024]{1,0:T(8,128)}) %all-reduce.3.cloned.1.call-update) | async-done | bytes 3145744 | tf_op jit(solution)/shard_map/psum | solution.py:117
  95.4 76.1 %all-reduce.4 = bf16[768,1024]{1,0:T(8,128)(2,1)} all-reduce(f32[768,1024]{1,0:T(8,128)} %all-reduce.3.cloned.1.call-done), channel_id=1, replica_groups=mesh['grp'=2,'mr'=16,'mc'=8] {'mr'}, use_global_device_ids=true, to_apply=%region_4.7 | all-reduce | flops 786432 | bytes 4718592 | tf_op jit(solution)/shard_map/psum | solution.py:117
  171.5 1.8 multiply_reduce_fusion
  173.5 3.9 %fusion.18 = f32[768,896]{1,0:T(8,128)S(1)} fusion(bf16[768,1024]{1,0:T(8,128)(2,1)} %all-reduce.4, bf16[1024,896]{1,0:T(8,128)(2,1)} %param.25), kind=kOutput, calls=%fused_computation.55 | convolution fusion | flops 1409286144 | bytes 6160384 | tf_op jit(solution)/shard_map/dot_general | solution.py:123
  177.4 1.8 fusion.17
  179.2 2.9 pad_maximum_fusion
  182.1 1.4 constant_dynamic-slice_fusion
  183.6 106.4 %reduce-scatter.2.cloned.1.call-done = f32[96,1793]{1,0:T(8,128)} async-done(((f32[768,1793]{1,0:T(8,128)}), f32[96,1793]{1,0:T(8,128)}) %reduce-scatter.2.cloned.1.call-update) | async-done | bytes 688528 | tf_op jit(solution)/shard_map/reduce_scatter | solution.py:36
  290.0 0.9 fusion.9
  290.9 1.9 fusion.4
  (34 shorter events, 2.3 us)
Async XLA Ops:
  7.2 6.7 %copy-start = (bf16[24,512,128]{2,1,0:T(8,128)(2,1)S(1)}, bf16[24,512,128]{2,1,0:T(8,128)(2,1)}, u32[]{:S(2)}) copy-start(bf16[24,512,128]{2,1,0:T(8,128)(2,1)} %param.18) | copy-start | bytes 9437188
  13.6 1.9 copy-start.2
  36.8 23.7 %all-to-all-start.1 = ((bf16[24,32,256]{2,0,1:T(8,128)(2,1)}), bf16[24,32,256]{2,0,1:T(8,128)(2,1)S(1)}, u32[]{:S(2)}, u32[]{:S(2)}) async-start(bf16[24,32,256]{2,0,1:T(8,128)(2,1)} %copy.19), calls=%async_computation.1 | async-start | bytes 786432 | tf_op jit(solution)/shard_map/all_to_all | solution.py:111
  47.1 48.2 %all-reduce.3.cloned.1.call-start = ((), (), s32[]{:S(2)}) async-start(), calls=%async_computation.3 | async-start | bytes 6291456 | tf_op jit(solution)/shard_map/psum | solution.py:117
  60.5 3.3 %copy-start.3 = (bf16[24,1024]{1,0:T(8,128)(2,1)S(1)}, bf16[24,1024]{1,0:T(8,128)(2,1)}, u32[]{:S(2)}) copy-start(bf16[24,1024]{1,0:T(8,128)(2,1)} %param.22) | copy-start | bytes 147460
  65.4 224.6 %reduce-scatter.2.cloned.1.call-start = ((), (), s32[]{:S(2)}) async-start(), calls=%async_computation.4 | async-start | bytes 6635520 | tf_op jit(solution)/shard_map/reduce_scatter | solution.py:36
  173.5 3.9 %copy-start.1 = (bf16[768,1024]{1,0:T(8,128)(2,1)S(1)}, bf16[768,1024]{1,0:T(8,128)(2,1)}, u32[]{:S(2)}) copy-start(bf16[768,1024]{1,0:T(8,128)(2,1)} %all-reduce.4) | copy-start | bytes 4718596
  173.5 3.9 %copy-start.4 = (bf16[1024,896]{1,0:T(8,128)(2,1)S(1)}, bf16[1024,896]{1,0:T(8,128)(2,1)}, u32[]{:S(2)}) copy-start(bf16[1024,896]{1,0:T(8,128)(2,1)} %param.24) | copy-start | bytes 5505028
Sparse Core Ops, SparseCore 0:
  65.5 29.8 all-reduce.2
  182.3 107.6 reduce-scatter.1
